TPU v7x, 32 devices: a whole 2x2x4 slice. The times are simulated.
32 devices in a mesh: dp: 16 (over z, y, x), mp: 2 (over core).
Axes of the slice: x: 2, y: 2, z: 4, core: 2. Of those that a mesh axis runs over, the one named last changes fastest.
Arguments:
- gradient: bfloat16 [2, 8, 512, 512], P('mp', None, 'dp'), may hold values from -54 to 54
- owners: int32 [2, 8], P('mp'), may hold values from 0 to 15, as said below
- left_stats: float32 [2, 16, 512, 512], P('mp', 'dp'), may hold values from -0.2 to 20.2
- right_stats: float32 [2, 16, 512, 512], P('mp', 'dp'), may hold values from -0.2 to 20.2
- left_roots_old: bfloat16 [2, 16, 512, 512], P('mp', 'dp'), may hold values from -0.1 to 1.5
- right_roots_old: bfloat16 [2, 16, 512, 512], P('mp', 'dp'), may hold values from -0.1 to 1.5
Outputs:
- update: bfloat16 [2, 8, 512, 512], P('mp', None, 'dp')
- left_roots: bfloat16 [2, 16, 512, 512], P('mp', 'dp')
- right_roots: bfloat16 [2, 16, 512, 512], P('mp', 'dp')
Inputs may be any that keep to these rules, and one draw needn't show every extreme that they name: In each row the 8 owners are distinct. Owner o holds a block of row m exactly when owner (o + 8) mod 16 of row m holds none, and exactly when owner o of row (m + 1) mod 2 holds none.
All inputs are finite; a program needn't handle non-finite values.
Results may differ from a plain program's by a relative error of at most 0.0067.
Values may be sent and summed in bfloat16 or wider, within the bound.
A program may use at most 64 MiB of HBM per device.

v0:
```python
import jax
import jax.numpy as jnp
from jax import lax
from jax.sharding import PartitionSpec as P

ITERS = 2
stat_decay = 0.9
ridge_term = 0.001
tiny_term = 1e-06


def newton_root(statistic):
    dimension = statistic.shape[0]
    identity = jnp.eye(dimension, dtype=jnp.float32)
    shifted = statistic + ridge_term * identity
    norm_scale = jnp.sqrt(jnp.sum(shifted * shifted) + tiny_term)
    matrix = shifted / norm_scale
    iterate = identity
    for iteration in range(ITERS):
        factor = ((5.0 * identity - matrix) / 4.0).astype(jnp.bfloat16)
        if iteration == 0:
            iterate = norm_scale ** (-0.25) * lax.optimization_barrier(factor).astype(jnp.float32)
        else:
            iterate = jnp.dot(
                iterate.astype(jnp.bfloat16), factor, preferred_element_type=jnp.float32
            )
        if iteration + 1 < ITERS:
            factor_two = jnp.dot(factor, factor, preferred_element_type=jnp.float32).astype(
                jnp.bfloat16
            )
            factor_four = jnp.dot(
                factor_two, factor_two, preferred_element_type=jnp.float32
            ).astype(jnp.bfloat16)
            matrix = jnp.dot(
                factor_four, matrix.astype(jnp.bfloat16), preferred_element_type=jnp.float32
            )
    return iterate.astype(jnp.bfloat16)


def shards(gradient, owners, left_stats, right_stats, left_roots_old, right_roots_old):
    dp_count = lax.axis_size("dp")
    my_index = lax.axis_index("dp")
    blocks_here = gradient.shape[1]
    row_count = gradient.shape[2]
    block_width = gradient.shape[3]
    owner_table = owners[0]
    owner_ids = jnp.arange(dp_count, dtype=jnp.int32)
    selector = (owner_table[None, :] == owner_ids[:, None]).astype(jnp.bfloat16)
    flat_grad = gradient[0].reshape(blocks_here, row_count * block_width)
    outgoing = jnp.dot(selector, flat_grad, preferred_element_type=jnp.float32).astype(jnp.bfloat16)
    outgoing = outgoing.reshape(dp_count, row_count, block_width)
    arrived = lax.all_to_all(outgoing, "dp", split_axis=0, concat_axis=1, tiled=True)
    grad_block = arrived[0]
    is_mine = owner_table == my_index
    mine_weight = is_mine.astype(jnp.float32)
    is_busy = jnp.any(is_mine)
    left_gram = jnp.einsum("ik,jk->ij", grad_block, grad_block, preferred_element_type=jnp.float32)
    right_gram = jnp.einsum("ki,kj->ij", grad_block, grad_block, preferred_element_type=jnp.float32)
    left_new = stat_decay * left_stats[0, 0] + left_gram / block_width
    right_new = stat_decay * right_stats[0, 0] + right_gram / block_width
    shaded = jnp.dot(grad_block, right_roots_old[0, 0], preferred_element_type=jnp.float32).astype(
        jnp.bfloat16
    )
    direction = jnp.dot(left_roots_old[0, 0], shaded, preferred_element_type=jnp.float32).astype(
        jnp.bfloat16
    )
    squares = jnp.stack(
        [
            jnp.sum(jnp.square(grad_block.astype(jnp.float32))),
            jnp.sum(jnp.square(direction.astype(jnp.float32))),
        ]
    )
    graft_terms = squares[:, None] * mine_weight[None, :]
    returned = lax.all_to_all(direction[None], "dp", split_axis=1, concat_axis=0, tiled=True)
    totals = lax.psum(graft_terms, ("dp", "mp"))
    graft_scale = jnp.sqrt(totals[0] / (totals[1] + tiny_term))
    pieces = jnp.einsum(
        "on,or->nr",
        selector,
        returned.reshape(dp_count, row_count * block_width),
        preferred_element_type=jnp.float32,
    )
    update = (
        (graft_scale[:, None] * pieces)
        .astype(jnp.bfloat16)
        .reshape(1, blocks_here, row_count, block_width)
    )
    zero_root = jnp.zeros((block_width, block_width), jnp.bfloat16)
    left_root, right_root = lax.cond(
        is_busy,
        lambda: (newton_root(left_new), newton_root(right_new)),
        lambda: (zero_root, zero_root),
    )
    return (update, left_root[None, None], right_root[None, None])


def solution(mesh):
    return jax.shard_map(
        shards,
        mesh=mesh,
        in_specs=(
            P("mp", None, "dp", None),
            P("mp", None),
            P("mp", "dp", None, None),
            P("mp", "dp", None, None),
            P("mp", "dp", None, None),
            P("mp", "dp", None, None),
        ),
        out_specs=(P("mp", None, "dp", None), P("mp", "dp", None, None), P("mp", "dp", None, None)),
        check_vma=False,
    )
```

profile of v0, /device:TPU:0, one launch (start us, length us, event | category | flops | bytes accessed | tf_op | source)
XLA Modules:
  0.0 111.4 jit_solution(4444039082128814350)
XLA Ops:
  0.6 0.0 copy-start
  0.6 1.2 %copy.18 = bf16[1,8,32,512]{3,1,2,0:T(8,128)(2,1)S(1)} copy(bf16[1,8,32,512]{3,2,1,0:T(8,128)(2,1)} %param.8) | data formatting | bytes 524288
  1.8 0.0 copy-start.4
  1.8 0.6 copy-done.4
  2.5 0.3 convolution_convert_fusion.6
  2.7 1.0 copy.19
  3.7 0.0 copy-start.5
  3.7 8.5 %all-to-all-start = ((bf16[16,32,512]{2,1,0:T(8,128)(2,1)}), bf16[16,32,512]{2,1,0:T(8,128)(2,1)S(1)}, u32[]{:S(2)}, u32[]{:S(2)}) async-start(bf16[16,32,512]{2,1,0:T(8,128)(2,1)} %bitcast.21), calls=%async_computation | async-start | bytes 1048576 | tf_op jit(solution)/shard_map/all_to_all | solution.py:52
  12.2 0.6 compare_reduce_fusion
  12.8 14.4 %all-to-all-done = bf16[16,32,512]{2,1,0:T(8,128)(2,1)S(1)} async-done(((bf16[16,32,512]{2,1,0:T(8,128)(2,1)}), bf16[16,32,512]{2,1,0:T(8,128)(2,1)S(1)}, u32[]{:S(2)}, u32[]{:S(2)}) %all-to-all-start) | async-done | bytes 524320 | tf_op jit(solution)/shard_map/all_to_all | solution.py:52
  27.3 0.0 copy-done
  27.3 0.0 copy-done.5
  27.3 1.5 %multiply_reduce_fusion.2 = (f32[]{:T(128)}, bf16[512,512]{1,0:T(8,128)(2,1)S(1)}) fusion(bf16[1,1,512,512]{3,2,1,0:T(8,128)(2,1)S(1)} %copy-done, bf16[512,512]{1,0:T(8,128)(2,1)S(1)} %bitcast.76, bf16[1,1,512,512]{3,2,1,0:T(8,128)(2,1)S(1)} %copy-done.5), kind=kOutput, calls=%fused_computation.53 | convolution fusion | flops 538181632 | bytes 2097156 | tf_op jit(solution)/shard_map/dot_general | solution.py:64
  28.8 0.9 copy.16
  29.7 0.5 broadcast.160
  30.2 3.8 %reduce.3 = bf16[512,512]{1,0:T(8,128)(2,1)S(1)} reduce(bf16[512,1,512]{2,1,0:T(2,128)(2,1)S(1)} %bitcast.78, bf16[]{:T(256)} %broadcast.160), dimensions={1}, to_apply=%bitcast.56.reduce_sub_computation | reduce | bytes 1048578
  34.0 1.2 %reshape.49 = bf16[16,2,8192]{2,1,0:T(2,128)(2,1)} reshape(bf16[512,512]{1,0:T(8,128)(2,1)S(1)} %reduce.3) | data formatting | bytes 1048576
  35.2 4.2 %all-to-all-start.1 = ((bf16[16,2,8192]{2,1,0:T(2,128)(2,1)}), bf16[16,2,8192]{2,1,0:T(2,128)(2,1)}, u32[]{:S(2)}, u32[]{:S(2)}) async-start(bf16[16,2,8192]{2,1,0:T(2,128)(2,1)} %reshape.49), calls=%async_computation.1 | async-start | bytes 1048576 | tf_op jit(solution)/shard_map/all_to_all | solution.py:74
  39.5 0.9 multiply_reduce_fusion.3
  40.3 1.4 %pad_maximum_fusion = f32[2]{0:T(128)S(1)} fusion(f32[1]{0:T(128)} %bitcast.6, f32[1]{0:T(128)} %bitcast.1), kind=kLoop, calls=%fused_computation.63 | loop fusion | flops 2 | bytes 16 | tf_op jit(solution)/shard_map/stack | solution.py:67
  41.7 0.1 broadcast_multiply_fusion
  42.4 40.7 %psum.7 = f32[2,8]{1,0:T(2,128)S(1)} all-reduce(f32[2,8]{1,0:T(2,128)S(1)} %broadcast_multiply_fusion), channel_id=1, replica_groups=mesh['dp'=16,'mp'=2] {'dp','mp'}, use_global_device_ids=true, to_apply=%region_2.0 | all-reduce | flops 16 | bytes 128 | tf_op jit(solution)/shard_map/psum | solution.py:75
  83.1 0.5 fusion.37
  83.6 0.0 copy-start.1
  83.6 1.5 %convolution_bitcast_fusion = f32[512,512]{1,0:T(8,128)} fusion(bf16[16,32,512]{2,1,0:T(8,128)(2,1)S(1)} %all-to-all-done), kind=kOutput, calls=%fused_computation.50 | convolution fusion | flops 268435456 | bytes 1572864 | tf_op jit(solution)/shard_map/ki,kj->ij/dot_general | solution.py:58
  85.1 0.0 copy-done.1
  85.1 18.9 %conditional.1 = (bf16[1,1,512,512]{3,2,1,0:T(8,128)(2,1)S(1)}, bf16[1,1,512,512]{3,2,1,0:T(8,128)(2,1)}) conditional(s32[]{:T(128)} %convert_element_type.101, () %tuple.22, (f32[1,1,512,512]{3,2,1,0:T(8,128)S(1)}, f32[512,512]{1,0:T(8,128)S(1)}, f32[1,1,512,512]{3,2,1,0:T(8,128)}, f32[512,512]{1,0:T(8,128)}) %tuple.39), branch_computations={%region_4.0_spmd, %region_5.0_spmd.clone} | conditional | flops 2166620160 | bytes 20971660 | solution.py:89
  85.1 0.9 multiply_reduce_fusion.1
  86.7 2.4 %multiply_reduce_fusion = f32[]{:T(128)} fusion(f32[512,512]{1,0:T(8,128)} %get-tuple-element.58, f32[1,1,512,512]{3,2,1,0:T(8,128)} %get-tuple-element.60), kind=kLoop, calls=%fused_computation.25 | loop fusion | flops 2097151 | bytes 2097156 | tf_op jit(solution)/shard_map/cond/branch_1_fun/reduce_sum | solution.py:16
  89.8 2.9 %fusion.7 = (bf16[512,512]{1,0:T(8,128)(2,1)S(1)}, bf16[512,512]{1,0:T(8,128)(2,1)}) fusion(f32[]{:T(128)S(6)} %sqrt.20, f32[512,512]{1,0:T(8,128)S(1)} %get-tuple-element.57, f32[1,1,512,512]{3,2,1,0:T(8,128)S(1)} %get-tuple-element.59, f32[]{:T(128)S(6)} %sqrt.21, f32[512,512]{1,0:T(8,128)} %get-tuple-element.58, f32[1,1,512,512]{3,2,1,0:T(8,128)} %get-tuple-element.60), kind=kLoop, calls=%fused_computation.19 | loop fusion | flops 4980736 | bytes 5242888 | tf_op jit(solution)/shard_map/cond/branch_1_fun/convert_element_type | solution.py:20
  92.7 0.0 copy-start.3
  92.7 3.6 %convolution_convert_fusion.1 = bf16[512,512]{1,0:T(8,128)(2,1)} fusion(bf16[512,512]{1,0:T(8,128)(2,1)} %get-tuple-element.75), kind=kOutput, calls=%fused_computation.9 | convolution fusion | flops 537395200 | bytes 1048576 | tf_op jit(solution)/shard_map/cond/branch_1_fun/dot_general | solution.py:31
  96.4 3.5 %fusion.5 = bf16[1,1,512,512]{3,2,1,0:T(8,128)(2,1)} fusion(bf16[512,512]{1,0:T(8,128)(2,1)} %convolution_convert_fusion.1, bf16[512,512]{1,0:T(8,128)(2,1)} %get-tuple-element.75, f32[]{:T(128)S(6)} %pow.9, f32[]{:T(128)S(6)} %sqrt.21, f32[1,1,512,512]{3,2,1,0:T(8,128)} %get-tuple-element.60, f32[512,512]{1,0:T(8,128)} %get-tuple-element.58), kind=kOutput, calls=%fused_computation.17 | convolution fusion | flops 541327360 | bytes 3670024 | tf_op jit(solution)/shard_map/cond/branch_1_fun/dot_general | solution.py:24
  99.9 0.0 copy-done.3
  99.9 1.8 %convolution_convert_fusion.4 = bf16[512,512]{1,0:T(8,128)(2,1)} fusion(bf16[512,512]{1,0:T(8,128)(2,1)S(1)} %get-tuple-element.74), kind=kOutput, calls=%fused_computation.12 | convolution fusion | flops 537395200 | bytes 1048576 | tf_op jit(solution)/shard_map/cond/branch_1_fun/dot_general | solution.py:31
  101.8 2.1 %fusion.4 = bf16[1,1,512,512]{3,2,1,0:T(8,128)(2,1)S(1)} fusion(bf16[512,512]{1,0:T(8,128)(2,1)} %convolution_convert_fusion.4, bf16[512,512]{1,0:T(8,128)(2,1)} %copy-done.3, f32[]{:T(128)S(6)} %pow.8, f32[]{:T(128)S(6)} %sqrt.20, f32[1,1,512,512]{3,2,1,0:T(8,128)S(1)} %get-tuple-element.59, f32[512,512]{1,0:T(8,128)S(1)} %get-tuple-element.57), kind=kOutput, calls=%fused_computation.16 | convolution fusion | flops 541327360 | bytes 3670024 | tf_op jit(solution)/shard_map/cond/branch_1_fun/dot_general | solution.py:24
  104.0 0.0 copy-start.2
  104.0 0.8 copy-done.2
  104.8 0.0 all-to-all-done.1
  104.8 2.2 %reshape.50 = bf16[512,1,512]{2,1,0:T(2,128)(2,1)S(1)} reshape(bf16[16,2,8192]{2,1,0:T(2,128)(2,1)} %all-to-all-done.1) | data formatting | bytes 1048576
  107.0 3.1 %bitcast_reduce_fusion = bf16[512,512]{1,0:T(8,128)(2,1)S(1)} fusion(bf16[512,1,512]{2,1,0:T(2,128)(2,1)S(1)} %reshape.50), kind=kLoop, calls=%fused_computation.67 | loop fusion | bytes 1048576 | tf_op jit(solution)/shard_map/all_to_all | solution.py:74
  110.1 0.2 reshape.40
  110.4 0.3 fusion.28
  110.7 0.8 copy.17
  (2 shorter events, 0.0 us)
Async XLA Ops:
  0.6 26.6 %copy-start = (bf16[1,1,512,512]{3,2,1,0:T(8,128)(2,1)S(1)}, bf16[1,1,512,512]{3,2,1,0:T(8,128)(2,1)}, u32[]{:S(2)}) copy-start(bf16[1,1,512,512]{3,2,1,0:T(8,128)(2,1)} %param.12) | copy-start | bytes 1572868
  1.8 0.7 copy-start.4
  3.7 23.6 %copy-start.5 = (bf16[1,1,512,512]{3,2,1,0:T(8,128)(2,1)S(1)}, bf16[1,1,512,512]{3,2,1,0:T(8,128)(2,1)}, u32[]{:S(2)}) copy-start(bf16[1,1,512,512]{3,2,1,0:T(8,128)(2,1)} %param.13) | copy-start | bytes 1572868
  3.7 23.6 %all-to-all-start = ((bf16[16,32,512]{2,1,0:T(8,128)(2,1)}), bf16[16,32,512]{2,1,0:T(8,128)(2,1)S(1)}, u32[]{:S(2)}, u32[]{:S(2)}) async-start(bf16[16,32,512]{2,1,0:T(8,128)(2,1)} %bitcast.21), calls=%async_computation | async-start | bytes 1048576 | tf_op jit(solution)/shard_map/all_to_all | solution.py:52
  35.2 69.6 %all-to-all-start.1 = ((bf16[16,2,8192]{2,1,0:T(2,128)(2,1)}), bf16[16,2,8192]{2,1,0:T(2,128)(2,1)}, u32[]{:S(2)}, u32[]{:S(2)}) async-start(bf16[16,2,8192]{2,1,0:T(2,128)(2,1)} %reshape.49), calls=%async_computation.1 | async-start | bytes 1048576 | tf_op jit(solution)/shard_map/all_to_all | solution.py:74
  83.6 1.5 %copy-start.1 = (f32[1,1,512,512]{3,2,1,0:T(8,128)S(1)}, f32[1,1,512,512]{3,2,1,0:T(8,128)}, u32[]{:S(2)}) copy-start(f32[1,1,512,512]{3,2,1,0:T(8,128)} %param.10) | copy-start | bytes 3145732
  92.7 7.2 %copy-start.3 = (bf16[512,512]{1,0:T(8,128)(2,1)}, bf16[512,512]{1,0:T(8,128)(2,1)S(1)}, u32[]{:S(2)}) copy-start(bf16[512,512]{1,0:T(8,128)(2,1)S(1)} %get-tuple-element.74) | copy-start | bytes 1572868 | tf_op jit(solution)/shard_map/cond
  104.0 0.8 copy-start.2
where the time goes:
time: 112 us; the launch traced here: 111 us
  blocking collectives  40.7 us (36%)
  matrix products  15 us (13%)
  waiting for transfers between devices  14.4 us (13%)
  other arithmetic  13 us (12%)
  starting transfers between devices  12.7 us (11%)
  local copies, waits for them, and re-layouts  12.5 us (11%)
  loops' own time  1.68 us (2%)
  between operations  1.41 us (1%)
    psum x1, blocking collectives, shards(): totals = lax.psum(graft_terms, ('dp', 'mp'))  40.7 us
    all_to_all x1, waiting for transfers between devices, shards(): lax.all_to_all(outgoing, 'dp', split_axis=0, concat_axis=1, tiled=True)  14.4 us
    all_to_all x1, starting transfers between devices, shards(): lax.all_to_all(outgoing, 'dp', split_axis=0, concat_axis=1, tiled=True)  8.47 us
    unnamed x16, local copies, waits for them, and re-layouts  8.25 us
    dot_general x2, matrix products, newton_root(): jnp.dot(iterate.astype(jnp.bfloat16), factor, preferred_element_type=jnp....  5.58 us
    dot_general x2, matrix products, newton_root(): jnp.dot(factor_two, factor_two, preferred_element_type=jnp.float32)  5.42 us
    all_to_all x1, starting transfers between devices, shards(): lax.all_to_all(direction[None], 'dp', split_axis=1, concat_axis=0, tiled=...  4.23 us
    unnamed x1, other arithmetic  3.82 us
  transfers between devices with their start and end apart: 2, of which 1 were waited for; matrix products, arithmetic and copies ran while one was open for 20% of the time, Pallas kernels for 0%

commit v1 on v0

--- a/solution.py
+++ b/solution.py
@@ -72,7 +72,7 @@
     )
     graft_terms = squares[:, None] * mine_weight[None, :]
     returned = lax.all_to_all(direction[None], "dp", split_axis=1, concat_axis=0, tiled=True)
-    totals = lax.psum(graft_terms, ("dp", "mp"))
+    totals = lax.psum(lax.psum(graft_terms, "mp"), "dp")
     graft_scale = jnp.sqrt(totals[0] / (totals[1] + tiny_term))
     pieces = jnp.einsum(
         "on,or->nr",

time: 112 us -> 118 us (1.054)
  blocking collectives: 40.7 us -> 44.6 us
  matrix products: 15 us -> 17.6 us
    psum x1 -> x2, blocking collectives: 40.7 us -> 44.6 us  [shards(): totals = lax.psum(lax.psum(graft_terms, 'mp'), 'dp')]
    dot_general x2, matrix products: 5.42 us -> 7.18 us  [newton_root(): jnp.dot(factor_two, factor_two, preferred_element_type=jnp.float32)]
    unnamed x16 -> x14, local copies, waits for them, and re-layouts: 8.25 us -> 8.24 us
  transfers between devices with their start and end apart: 2 -> 2, of which waited for: 1 -> 1; matrix products, arithmetic and copies ran while one was open for 20% -> 21% of each run, Pallas kernels for 0% -> 0%
where the time goes in v1:
time: 118 us; the launch traced here: 117 us
  blocking collectives  44.6 us (38%)
  matrix products  17.6 us (15%)
  waiting for transfers between devices  13.8 us (12%)
  other arithmetic  13.3 us (11%)
  starting transfers between devices  12.7 us (11%)
  local copies, waits for them, and re-layouts  12.4 us (11%)
  loops' own time  1.5 us (1%)
  between operations  1.39 us (1%)
    psum x2, blocking collectives, shards(): totals = lax.psum(lax.psum(graft_terms, 'mp'), 'dp')  44.6 us
    all_to_all x1, waiting for transfers between devices, shards(): lax.all_to_all(outgoing, 'dp', split_axis=0, concat_axis=1, tiled=True)  13.8 us
    all_to_all x1, starting transfers between devices, shards(): lax.all_to_all(outgoing, 'dp', split_axis=0, concat_axis=1, tiled=True)  8.47 us
    unnamed x14, local copies, waits for them, and re-layouts  8.24 us
    dot_general x2, matrix products, newton_root(): jnp.dot(factor_two, factor_two, preferred_element_type=jnp.float32)  7.18 us
    dot_general x2, matrix products, newton_root(): jnp.dot(iterate.astype(jnp.bfloat16), factor, preferred_element_type=jnp....  6.38 us
    all_to_all x1, starting transfers between devices, shards(): lax.all_to_all(direction[None], 'dp', split_axis=1, concat_axis=0, tiled=...  4.23 us
    unnamed x1, other arithmetic  3.82 us
  transfers between devices with their start and end apart: 2, of which 1 were waited for; matrix products, arithmetic and copies ran while one was open for 21% of the time, Pallas kernels for 0%

profile of v1, /device:TPU:0, one launch (start us, length us, event | category | flops | bytes accessed | tf_op | source)
XLA Modules:
  0.0 117.3 jit_solution(14797833556148512014)
XLA Ops:
  0.6 0.0 copy-start
  0.6 1.2 copy.18
  1.8 0.0 copy-start.2
  1.8 0.6 copy-done.2
  2.5 0.3 convolution_convert_fusion.6
  2.7 1.0 copy.19
  3.7 0.0 copy-start.3
  3.7 8.5 %all-to-all-start = ((bf16[16,32,512]{2,1,0:T(8,128)(2,1)}), bf16[16,32,512]{2,1,0:T(8,128)(2,1)S(1)}, u32[]{:S(2)}, u32[]{:S(2)}) async-start(bf16[16,32,512]{2,1,0:T(8,128)(2,1)} %bitcast.21), calls=%async_computation | async-start | bytes 1048576 | tf_op jit(solution)/shard_map/all_to_all | solution.py:52
  12.2 0.6 compare_reduce_fusion
  13.5 13.8 %all-to-all-done = bf16[16,32,512]{2,1,0:T(8,128)(2,1)S(1)} async-done(((bf16[16,32,512]{2,1,0:T(8,128)(2,1)}), bf16[16,32,512]{2,1,0:T(8,128)(2,1)S(1)}, u32[]{:S(2)}, u32[]{:S(2)}) %all-to-all-start) | async-done | bytes 524320 | tf_op jit(solution)/shard_map/all_to_all | solution.py:52
  27.3 0.0 copy-done
  27.3 0.0 copy-done.3
  27.3 1.5 %multiply_reduce_fusion.2 = (f32[]{:T(128)}, bf16[512,512]{1,0:T(8,128)(2,1)S(1)}) fusion(bf16[1,1,512,512]{3,2,1,0:T(8,128)(2,1)S(1)} %copy-done, bf16[512,512]{1,0:T(8,128)(2,1)S(1)} %bitcast.76, bf16[1,1,512,512]{3,2,1,0:T(8,128)(2,1)S(1)} %copy-done.3), kind=kOutput, calls=%fused_computation.53 | convolution fusion | flops 538181632 | bytes 2097156 | tf_op jit(solution)/shard_map/dot_general | solution.py:64
  28.8 0.9 copy.16
  29.7 0.5 broadcast.160
  30.2 3.8 %reduce.3 = bf16[512,512]{1,0:T(8,128)(2,1)S(1)} reduce(bf16[512,1,512]{2,1,0:T(2,128)(2,1)S(1)} %bitcast.78, bf16[]{:T(256)} %broadcast.160), dimensions={1}, to_apply=%bitcast.56.reduce_sub_computation | reduce | bytes 1048578
  34.0 1.2 %reshape.49 = bf16[16,2,8192]{2,1,0:T(2,128)(2,1)} reshape(bf16[512,512]{1,0:T(8,128)(2,1)S(1)} %reduce.3) | data formatting | bytes 1048576
  35.2 4.2 %all-to-all-start.1 = ((bf16[16,2,8192]{2,1,0:T(2,128)(2,1)}), bf16[16,2,8192]{2,1,0:T(2,128)(2,1)}, u32[]{:S(2)}, u32[]{:S(2)}) async-start(bf16[16,2,8192]{2,1,0:T(2,128)(2,1)} %reshape.49), calls=%async_computation.1 | async-start | bytes 1048576 | tf_op jit(solution)/shard_map/all_to_all | solution.py:74
  39.5 1.5 %convolution_bitcast_fusion = f32[512,512]{1,0:T(8,128)} fusion(bf16[16,32,512]{2,1,0:T(8,128)(2,1)S(1)} %all-to-all-done), kind=kOutput, calls=%fused_computation.50 | convolution fusion | flops 268435456 | bytes 1572864 | tf_op jit(solution)/shard_map/ki,kj->ij/dot_general | solution.py:58
  40.9 0.0 copy-start.1
  40.9 0.5 fusion.37
  41.4 0.8 copy-done.1
  42.1 21.5 %conditional.1 = (bf16[1,1,512,512]{3,2,1,0:T(8,128)(2,1)}, bf16[1,1,512,512]{3,2,1,0:T(8,128)(2,1)}) conditional(s32[]{:T(128)} %convert_element_type.101, () %tuple.22, (f32[1,1,512,512]{3,2,1,0:T(8,128)S(1)}, f32[512,512]{1,0:T(8,128)S(1)}, f32[1,1,512,512]{3,2,1,0:T(8,128)}, f32[512,512]{1,0:T(8,128)}) %tuple.39), branch_computations={%region_5.0_spmd, %region_6.0_spmd.clone} | conditional | flops 2166620160 | bytes 18874480 | solution.py:89
  42.1 0.9 multiply_reduce_fusion.1
  43.8 2.4 %multiply_reduce_fusion = f32[]{:T(128)} fusion(f32[512,512]{1,0:T(8,128)} %get-tuple-element.58, f32[1,1,512,512]{3,2,1,0:T(8,128)} %get-tuple-element.60), kind=kLoop, calls=%fused_computation.25 | loop fusion | flops 2097151 | bytes 2097156 | tf_op jit(solution)/shard_map/cond/branch_1_fun/reduce_sum | solution.py:16
  46.9 3.1 %fusion.7 = (bf16[512,512]{1,0:T(8,128)(2,1)}, bf16[512,512]{1,0:T(8,128)(2,1)}) fusion(f32[]{:T(128)S(6)} %sqrt.20, f32[512,512]{1,0:T(8,128)S(1)} %get-tuple-element.57, f32[1,1,512,512]{3,2,1,0:T(8,128)S(1)} %get-tuple-element.59, f32[]{:T(128)S(6)} %sqrt.21, f32[512,512]{1,0:T(8,128)} %get-tuple-element.58, f32[1,1,512,512]{3,2,1,0:T(8,128)} %get-tuple-element.60), kind=kLoop, calls=%fused_computation.19 | loop fusion | flops 4980736 | bytes 5242888 | tf_op jit(solution)/shard_map/cond/branch_1_fun/convert_element_type | solution.py:20
  50.0 3.7 %convolution_convert_fusion.1 = bf16[512,512]{1,0:T(8,128)(2,1)} fusion(bf16[512,512]{1,0:T(8,128)(2,1)} %get-tuple-element.75), kind=kOutput, calls=%fused_computation.9 | convolution fusion | flops 537395200 | bytes 1048576 | tf_op jit(solution)/shard_map/cond/branch_1_fun/dot_general | solution.py:31
  53.7 3.5 %fusion.5 = bf16[1,1,512,512]{3,2,1,0:T(8,128)(2,1)} fusion(bf16[512,512]{1,0:T(8,128)(2,1)} %convolution_convert_fusion.1, bf16[512,512]{1,0:T(8,128)(2,1)} %get-tuple-element.75, f32[]{:T(128)S(6)} %pow.9, f32[]{:T(128)S(6)} %sqrt.21, f32[1,1,512,512]{3,2,1,0:T(8,128)} %get-tuple-element.60, f32[512,512]{1,0:T(8,128)} %get-tuple-element.58), kind=kOutput, calls=%fused_computation.17 | convolution fusion | flops 541327360 | bytes 3670024 | tf_op jit(solution)/shard_map/cond/branch_1_fun/dot_general | solution.py:24
  57.2 3.5 %convolution_convert_fusion.4 = bf16[512,512]{1,0:T(8,128)(2,1)} fusion(bf16[512,512]{1,0:T(8,128)(2,1)} %get-tuple-element.74), kind=kOutput, calls=%fused_computation.12 | convolution fusion | flops 537395200 | bytes 1048576 | tf_op jit(solution)/shard_map/cond/branch_1_fun/dot_general | solution.py:31
  60.8 2.9 %fusion.4 = bf16[1,1,512,512]{3,2,1,0:T(8,128)(2,1)} fusion(bf16[512,512]{1,0:T(8,128)(2,1)} %convolution_convert_fusion.4, bf16[512,512]{1,0:T(8,128)(2,1)} %get-tuple-element.74, f32[]{:T(128)S(6)} %pow.8, f32[]{:T(128)S(6)} %sqrt.20, f32[1,1,512,512]{3,2,1,0:T(8,128)S(1)} %get-tuple-element.59, f32[512,512]{1,0:T(8,128)S(1)} %get-tuple-element.57), kind=kOutput, calls=%fused_computation.16 | convolution fusion | flops 541327360 | bytes 3670024 | tf_op jit(solution)/shard_map/cond/branch_1_fun/dot_general | solution.py:24
  63.6 0.9 multiply_reduce_fusion.3
  64.6 1.4 %pad_maximum_fusion = f32[2]{0:T(128)S(1)} fusion(f32[1]{0:T(128)} %bitcast.6, f32[1]{0:T(128)} %bitcast.1), kind=kLoop, calls=%fused_computation.63 | loop fusion | flops 2 | bytes 16 | tf_op jit(solution)/shard_map/stack | solution.py:67
  66.0 0.1 broadcast_multiply_fusion
  66.1 2.4 %psum.14 = f32[2,8]{1,0:T(2,128)S(1)} all-reduce(f32[2,8]{1,0:T(2,128)S(1)} %broadcast_multiply_fusion), channel_id=1, replica_groups=mesh['dp'=16,'mp'=2] {'mp'}, use_global_device_ids=true, to_apply=%region_2.0 | all-reduce | flops 16 | bytes 128 | tf_op jit(solution)/shard_map/psum | solution.py:75
  68.5 42.1 %psum.15 = f32[2,8]{1,0:T(2,128)S(1)} all-reduce(f32[2,8]{1,0:T(2,128)S(1)} %psum.14), channel_id=1, replica_groups=mesh['dp'=16,'mp'=2] {'dp'}, use_global_device_ids=true, to_apply=%region_3.0 | all-reduce | flops 16 | bytes 128 | tf_op jit(solution)/shard_map/psum | solution.py:75
  110.7 0.0 all-to-all-done.1
  110.7 2.2 %reshape.50 = bf16[512,1,512]{2,1,0:T(2,128)(2,1)S(1)} reshape(bf16[16,2,8192]{2,1,0:T(2,128)(2,1)} %all-to-all-done.1) | data formatting | bytes 1048576
  112.9 3.1 %bitcast_reduce_fusion = bf16[512,512]{1,0:T(8,128)(2,1)S(1)} fusion(bf16[512,1,512]{2,1,0:T(2,128)(2,1)S(1)} %reshape.50), kind=kLoop, calls=%fused_computation.67 | loop fusion | bytes 1048576 | tf_op jit(solution)/shard_map/all_to_all | solution.py:74
  116.0 0.2 reshape.40
  116.2 0.3 fusion.28
  116.5 0.8 copy.17
  (2 shorter events, 0.0 us)
Async XLA Ops:
  0.6 26.6 %copy-start = (bf16[1,1,512,512]{3,2,1,0:T(8,128)(2,1)S(1)}, bf16[1,1,512,512]{3,2,1,0:T(8,128)(2,1)}, u32[]{:S(2)}) copy-start(bf16[1,1,512,512]{3,2,1,0:T(8,128)(2,1)} %param.12) | copy-start | bytes 1572868
  1.8 0.7 copy-start.2
  3.7 23.6 %copy-start.3 = (bf16[1,1,512,512]{3,2,1,0:T(8,128)(2,1)S(1)}, bf16[1,1,512,512]{3,2,1,0:T(8,128)(2,1)}, u32[]{:S(2)}) copy-start(bf16[1,1,512,512]{3,2,1,0:T(8,128)(2,1)} %param.13) | copy-start | bytes 1572868
  3.7 23.6 %all-to-all-start = ((bf16[16,32,512]{2,1,0:T(8,128)(2,1)}), bf16[16,32,512]{2,1,0:T(8,128)(2,1)S(1)}, u32[]{:S(2)}, u32[]{:S(2)}) async-start(bf16[16,32,512]{2,1,0:T(8,128)(2,1)} %bitcast.21), calls=%async_computation | async-start | bytes 1048576 | tf_op jit(solution)/shard_map/all_to_all | solution.py:52
  35.2 75.5 %all-to-all-start.1 = ((bf16[16,2,8192]{2,1,0:T(2,128)(2,1)}), bf16[16,2,8192]{2,1,0:T(2,128)(2,1)}, u32[]{:S(2)}, u32[]{:S(2)}) async-start(bf16[16,2,8192]{2,1,0:T(2,128)(2,1)} %reshape.49), calls=%async_computation.1 | async-start | bytes 1048576 | tf_op jit(solution)/shard_map/all_to_all | solution.py:74
  40.9 1.2 %copy-start.1 = (f32[1,1,512,512]{3,2,1,0:T(8,128)S(1)}, f32[1,1,512,512]{3,2,1,0:T(8,128)}, u32[]{:S(2)}) copy-start(f32[1,1,512,512]{3,2,1,0:T(8,128)} %param.10) | copy-start | bytes 3145732
